TPU v7x, 32 devices: a whole 2x2x4 slice. The times are simulated.
32 devices in a mesh: groups: 2 (over y), nodes: 16 (over z, x, core).
Axes of the slice: x: 2, y: 2, z: 4, core: 2. Of those that a mesh axis runs over, the one named last changes fastest.
Arguments:
- grid: bfloat16 [4096, 512], P(('groups', 'nodes')), parts along dimension 0, may hold values from -6 to 6
- hidden: bfloat16 [8192, 512], P(('groups', 'nodes')), parts along dimension 0, may hold values from -6 to 6
- enc_nbr: int32 [4096, 32], P('nodes'), may hold values from 0 to 2047, as said below
- dec_nbr: int32 [2048, 3], P('nodes'), may hold values from 0 to 4095, as said below
- enc_qkv: bfloat16 [512, 1536], replicated, may hold values from -0.25 to 0.25
- enc_out: bfloat16 [512, 512], replicated, may hold values from -0.25 to 0.25
- proc_qkv: bfloat16 [512, 1536], replicated, may hold values from -0.25 to 0.25
- proc_out: bfloat16 [512, 512], replicated, may hold values from -0.25 to 0.25
- dec_qkv: bfloat16 [512, 1536], replicated, may hold values from -0.25 to 0.25
- dec_out: bfloat16 [512, 512], replicated, may hold values from -0.25 to 0.25
- mlp_in: bfloat16 [512, 2048], replicated, may hold values from -0.25 to 0.25
- mlp_out: bfloat16 [2048, 512], replicated, may hold values from -0.125 to 0.125
Outputs:
- grid_out: bfloat16 [4096, 512], P(('groups', 'nodes')), parts along dimension 0
- hidden_two: bfloat16 [8192, 512], P(('groups', 'nodes')), parts along dimension 0
There are 2 independent parts, one for each index of `groups`. A program takes and returns all parts, laid end to end along the dimension named above; an argument that names none is the same for every part. Nothing has to cross between parts.
Inputs may be any that keep to these rules, and one draw needn't show every extreme that they name: `enc_nbr`: row i names grid nodes of regions r - 1 to r + 1 only, with r = i // 256, region r holding grid nodes r * 128 to (r + 1) * 128 - 1. `dec_nbr`: row i names hidden nodes of regions r - 1 to r + 1 only, with r = i // 128, region r holding hidden nodes r * 256 to (r + 1) * 256 - 1.
All inputs are finite; a program needn't handle non-finite values.
Results may differ from a plain program's by a relative error of at most 0.015.
Values may be sent and summed in bfloat16 or wider, within the bound.
A program may use at most 64 MiB of HBM per device.

v0:
```python
import jax
import jax.numpy as jnp
from jax import lax
from jax.sharding import PartitionSpec as P

HEADS = 16


EPSILON = 1e-05


def padded(shard, sides, width):
    for axis, dim in sides:
        devices, length = (lax.axis_size(axis), shard.shape[dim])
        up = [(i, (i + 1) % devices) for i in range(devices - 1)]
        down = [(j, i) for i, j in up]
        last = lax.slice_in_dim(shard, length - width, length, axis=dim)
        leading = lax.slice_in_dim(shard, 0, width, axis=dim)
        before = lax.ppermute(last, axis, up)
        after = lax.ppermute(leading, axis, down)
        shard = jnp.concatenate([before, shard, after], axis=dim)
    return shard


def partner_2(shard, axis, stride):
    return lax.ppermute(shard, axis, [(i, i ^ 1 << stride) for i in range(lax.axis_size(axis))])


def layer_norm(values):
    values = values.astype(jnp.float32)
    center = values - jnp.mean(values, axis=-1, keepdims=True)
    spread = jnp.mean(center * center, axis=-1, keepdims=True)
    return (center * lax.rsqrt(spread + EPSILON)).astype(jnp.bfloat16)


def product(left, right):
    return jnp.dot(left, right, preferred_element_type=jnp.float32)


def list_counts(lists, column_count):
    columns = jnp.arange(column_count, dtype=jnp.int32)
    return jnp.sum((lists[:, :, None] == columns[None, None, :]).astype(jnp.float32), axis=1)


def dense_partial(queries, key_values, counts):
    row_count = queries.shape[0]
    column_count = key_values.shape[0]
    model_width = queries.shape[1]
    head_size = model_width // HEADS
    query_heads = queries.reshape(row_count, HEADS, head_size)
    key_heads = key_values[:, :model_width].reshape(column_count, HEADS, head_size)
    value_heads = (
        key_values[:, model_width:].astype(jnp.float32).reshape(column_count, HEADS, head_size)
    )
    scores = jnp.einsum("nhd,chd->hnc", query_heads, key_heads, preferred_element_type=jnp.float32)
    scores = scores / jnp.sqrt(jnp.float32(head_size))
    present = (counts > 0.0)[None, :, :]
    scores = jnp.where(present, scores, -1e30)
    maxima = jnp.max(scores, axis=-1)
    weights = counts[None, :, :] * jnp.exp(scores - maxima[:, :, None])
    totals = jnp.sum(weights, axis=-1)
    numerator = jnp.einsum("hnc,chd->hnd", weights, value_heads, preferred_element_type=jnp.float32)
    return (maxima, totals, numerator)


def dense_attend(queries, key_values, counts):
    maxima, totals, numerator = dense_partial(queries, key_values, counts)
    mixed = numerator / totals[:, :, None]
    return jnp.transpose(mixed, (1, 0, 2)).reshape(queries.shape)


def window_attend(queries, key_values):
    row_count = queries.shape[0]
    key_count = key_values.shape[0]
    model_width = queries.shape[1]
    head_size = model_width // HEADS
    query_heads = queries.reshape(row_count, HEADS, head_size)
    key_heads = key_values[:, :model_width].reshape(key_count, HEADS, head_size)
    value_heads = (
        key_values[:, model_width:].astype(jnp.float32).reshape(key_count, HEADS, head_size)
    )
    scores = jnp.einsum("nhd,whd->hnw", query_heads, key_heads, preferred_element_type=jnp.float32)
    weights = jax.nn.softmax(scores / jnp.sqrt(jnp.float32(head_size)), axis=-1)
    mixed = jnp.einsum("hnw,whd->hnd", weights, value_heads, preferred_element_type=jnp.float32)
    return jnp.transpose(mixed, (1, 0, 2)).reshape(row_count, model_width)


def local(
    grid,
    hidden,
    enc_nbr,
    dec_nbr,
    enc_qkv,
    enc_out,
    proc_qkv,
    proc_out,
    dec_qkv,
    dec_out,
    mlp_in,
    mlp_out,
):
    model_width = grid.shape[1]
    grid_rows = grid.shape[0]
    hidden_rows = hidden.shape[0]
    device_pos = lax.axis_index("nodes")
    grid_normed = layer_norm(grid)
    enc_queries = product(layer_norm(hidden), enc_qkv[:, :model_width]).astype(jnp.bfloat16)
    enc_pairs = product(grid_normed, enc_qkv[:, model_width:]).astype(jnp.bfloat16)
    padded_pairs = padded(enc_pairs, (("nodes", 0),), grid_rows)
    local_lists = enc_nbr - (device_pos - 1) * grid_rows
    counts = list_counts(local_lists, 3 * grid_rows)
    enc_mix = dense_attend(enc_queries, padded_pairs, counts).astype(jnp.bfloat16)
    hidden_one = (hidden.astype(jnp.float32) + product(enc_mix, enc_out)).astype(jnp.bfloat16)
    proc_all = product(layer_norm(hidden_one), proc_qkv).astype(jnp.bfloat16)
    window_pairs = proc_all[:, model_width:]
    partner = partner_2(window_pairs, "nodes", 0)
    lower_half = device_pos >> 0 & 1 == 0
    window_pairs = jnp.where(
        lower_half,
        jnp.concatenate([window_pairs, partner], axis=0),
        jnp.concatenate([partner, window_pairs], axis=0),
    )
    proc_mix = window_attend(proc_all[:, :model_width], window_pairs).astype(jnp.bfloat16)
    hidden_two = (hidden_one.astype(jnp.float32) + product(proc_mix, proc_out)).astype(jnp.bfloat16)
    dec_queries = product(grid_normed, dec_qkv[:, :model_width]).astype(jnp.bfloat16)
    padded_state = padded(hidden_two, (("nodes", 0),), hidden_rows)
    padded_hidden = product(layer_norm(padded_state), dec_qkv[:, model_width:]).astype(jnp.bfloat16)
    dec_local = dec_nbr - (device_pos - 1) * hidden_rows
    dec_counts = list_counts(dec_local, 3 * hidden_rows)
    dec_mix = dense_attend(dec_queries, padded_hidden, dec_counts).astype(jnp.bfloat16)
    grid_one = (grid.astype(jnp.float32) + product(dec_mix, dec_out)).astype(jnp.bfloat16)
    mlp_hidden = jax.nn.gelu(product(layer_norm(grid_one), mlp_in)).astype(jnp.bfloat16)
    grid_out = (grid_one.astype(jnp.float32) + product(mlp_hidden, mlp_out)).astype(jnp.bfloat16)
    return (grid_out, hidden_two)


def solution(mesh):
    return jax.shard_map(
        local,
        mesh=mesh,
        in_specs=(
            P(("groups", "nodes"), None),
            P(("groups", "nodes"), None),
            P("nodes", None),
            P("nodes", None),
            P(),
            P(),
            P(),
            P(),
            P(),
            P(),
            P(),
            P(),
        ),
        out_specs=(P(("groups", "nodes"), None), P(("groups", "nodes"), None)),
        check_vma=False,
    )
```

profile of v0, /device:TPU:1, one launch (start us, length us, event | category | flops | bytes accessed | tf_op | source)
XLA Modules:
  0.0 74.2 jit_solution(9442191251416237930)
XLA Ops:
  0.6 1.2 %convert_reduce_fusion.4 = f32[128]{0:T(128)S(1)} fusion(bf16[128,512]{1,0:T(8,128)(2,1)} %param.12), kind=kLoop, calls=%fused_computation.91 | loop fusion | flops 130944 | bytes 131584 | tf_op jit(solution)/shard_map/reduce_sum | solution.py:31
  1.8 1.1 %fusion.67 = f32[128]{0:T(128)S(1)} fusion(bf16[128,512]{1,0:T(8,128)(2,1)} %param.12, f32[128]{0:T(128)S(1)} %broadcast_multiply_fusion.4), kind=kLoop, calls=%fused_computation.94 | loop fusion | flops 262016 | bytes 132096 | tf_op jit(solution)/shard_map/reduce_sum | solution.py:32
  2.9 1.7 %convolution_convert_fusion.2 = bf16[128,1024]{1,0:T(8,128)(2,1)S(1)} fusion(bf16[512,1536]{1,0:T(8,128)(2,1)} %param.16, bf16[128,512]{1,0:T(8,128)(2,1)} %param.12, f32[128]{0:T(128)S(1)} %add_rsqrt_fusion.4, f32[128]{0:T(128)S(1)} %broadcast_multiply_fusion.4), kind=kOutput, calls=%fused_computation.45 | convolution fusion | flops 134610944 | bytes 1442816 | tf_op jit(solution)/shard_map/dot_general | solution.py:37
  4.6 1.9 %collective-permute-start.1 = (bf16[128,1024]{1,0:T(8,128)(2,1)S(1)}, bf16[128,1024]{1,0:T(8,128)(2,1)S(1)}, u32[]{:S(2)}, u32[]{:S(2)}) collective-permute-start(bf16[128,1024]{1,0:T(8,128)(2,1)S(1)} %convolution_convert_fusion.2), channel_id=1, source_target_pairs={{1,0},{2,1},{3,2},{4,3},{5,4},{6,5},{7,6},{8,7},{9,8},{10,9},{11,1... | collective-permute-start | bytes 786440 | tf_op jit(solution)/shard_map/ppermute | solution.py:20
  6.5 4.5 %collective-permute-start = (bf16[128,1024]{1,0:T(8,128)(2,1)S(1)}, bf16[128,1024]{1,0:T(8,128)(2,1)}, u32[]{:S(2)}, u32[]{:S(2)}) collective-permute-start(bf16[128,1024]{1,0:T(8,128)(2,1)S(1)} %convolution_convert_fusion.2), channel_id=1, source_target_pairs={{0,1},{1,2},{2,3},{3,4},{4,5},{5,6},{6,7},{7,8},{8,9},{9,10},{10,1... | collective-permute-start | bytes 786440 | tf_op jit(solution)/shard_map/ppermute | solution.py:19
  11.9 2.2 %convert_reduce_fusion = f32[256,384]{1,0:T(8,128)S(1)} fusion(s32[256,32]{1,0:T(8,128)S(1)} %copy.37), kind=kLoop, calls=%fused_computation | loop fusion | flops 9338880 | bytes 425984 | tf_op jit(solution)/shard_map/reduce_sum | solution.py:42
  14.1 1.1 %convert_reduce_fusion.3 = f32[256]{0:T(256)S(1)} fusion(bf16[256,512]{1,0:T(8,128)(2,1)} %param.13), kind=kLoop, calls=%fused_computation.77 | loop fusion | flops 261888 | bytes 263168 | tf_op jit(solution)/shard_map/reduce_sum | solution.py:31
  15.2 1.2 %fusion.56 = f32[256]{0:T(256)S(1)} fusion(bf16[256,512]{1,0:T(8,128)(2,1)} %param.13, f32[256]{0:T(256)S(1)} %broadcast_multiply_fusion.2), kind=kLoop, calls=%fused_computation.80 | loop fusion | flops 524032 | bytes 264192 | tf_op jit(solution)/shard_map/reduce_sum | solution.py:32
  16.3 1.5 %convolution_convert_fusion.3 = bf16[256,512]{1,0:T(8,128)(2,1)S(1)} fusion(bf16[512,1536]{1,0:T(8,128)(2,1)} %param.16, bf16[256,512]{1,0:T(8,128)(2,1)} %param.13, f32[256]{0:T(256)S(1)} %add_rsqrt_fusion.2, f32[256]{0:T(256)S(1)} %broadcast_multiply_fusion.2), kind=kOutput, calls=%fused_computation.46 | convolution fusion | flops 134873088 | bytes 1050624 | tf_op jit(solution)/shard_map/dot_general | solution.py:37
  18.7 1.0 %pad_maximum_fusion = bf16[384,1024]{1,0:T(8,128)(2,1)S(1)} fusion(bf16[128,1024]{1,0:T(8,128)(2,1)S(1)} %collective-permute-done.1, bf16[128,1024]{1,0:T(8,128)(2,1)S(1)} %convolution_convert_fusion.2, bf16[128,1024]{1,0:T(8,128)(2,1)} %collective-permute-done), kind=kLoop, calls=%fused_computation.72 | loop fusion | flops 2359296 | bytes 1572864 | tf_op jit(solution)/shard_map/concatenate | solution.py:21
  20.9 2.3 %fusion.3 = (f32[16,256]{1,0:T(8,128)S(1)}, f32[16,256,384]{2,1,0:T(8,128)S(1)}) fusion(pred[256,384]{1,0:T(8,128)(4,1)} %broadcast_compare_fusion, bf16[256,16,32]{0,2,1:T(8,128)(2,1)S(1)} %bitcast.49, bf16[384,16,32]{0,2,1:T(8,128)(2,1)S(1)} %bitcast.48), kind=kOutput, calls=%fused_computation.11 | convolution fusion | flops 105377792 | bytes 7061504 | tf_op jit(solution)/shard_map/nhd,chd->hnc/dot_general | solution.py:55
  23.2 2.1 %fusion.5 = f32[16,256]{1,0:T(8,128)S(1)} fusion(f32[16,256,384]{2,1,0:T(8,128)S(1)} %get-tuple-element.9, f32[16,256]{1,0:T(8,128)S(1)} %get-tuple-element.8, f32[256,384]{1,0:T(8,128)S(1)} %convert_reduce_fusion, pred[256,384]{1,0:T(8,128)(4,1)S(1)} %copy-done.7), kind=kLoop, calls=%fused_computation.13 | loop fusion | flops 7860224 | bytes 6815744 | tf_op jit(solution)/shard_map/reduce_sum | solution.py:61
  25.3 2.1 %fusion.50 = bf16[256,16,32]{0,2,1:T(8,128)(2,1)S(1)} fusion(bf16[384,16,32]{0,2,1:T(8,128)(2,1)S(1)} %bitcast.54, f32[16,256,384]{2,1,0:T(8,128)S(1)} %get-tuple-element.9, f32[16,256]{1,0:T(8,128)S(1)} %get-tuple-element.8, f32[256,384]{1,0:T(8,128)S(1)} %convert_reduce_fusion, pred[256,384]{1,0:T(8,128)(4,1)S(1)} %copy-done.7, f32[256,16]{0,1:T(8,128)S(1)} %bitcast.58), kind=kOutput, calls=%fused_computation.71 | convolution fusion | flops 107216896 | bytes 7471104 | tf_op jit(solution)/shard_map/hnc,chd->hnd/dot_general | solution.py:62
  29.6 2.0 %convolution_convert_fusion.4 = bf16[128,512]{1,0:T(8,128)(2,1)} fusion(bf16[512,1536]{1,0:T(8,128)(2,1)} %param.20, bf16[128,512]{1,0:T(8,128)(2,1)S(1)} %copy-done.4, f32[128]{0:T(128)S(1)} %add_rsqrt_fusion.4, f32[128]{0:T(128)S(1)} %broadcast_multiply_fusion.4), kind=kOutput, calls=%fused_computation.56 | convolution fusion | flops 67436544 | bytes 787456 | tf_op jit(solution)/shard_map/dot_general | solution.py:37
  32.3 1.1 %copy.41 = bf16[256,512]{0,1:T(8,128)(2,1)S(1)} copy(bf16[256,512]{1,0:T(8,128)(2,1)} %slice.50) | data formatting | bytes 524288 | tf_op jit(solution)/shard_map/slice | solution.py:123
  33.4 2.0 %maximum_select_fusion = bf16[512,1024]{1,0:T(8,128)(2,1)S(1)} fusion(bf16[256,1024]{1,0:T(8,128)(2,1)} %collective-permute-done.2, bf16[256,1024]{1,0:T(8,128)(2,1)} %slice.51, pred[]{:T(512)S(6)} %eq.35), kind=kLoop, calls=%fused_computation.67 | loop fusion | flops 4718592 | bytes 2097153 | tf_op jit(solution)/shard_map/jit(_where)/select_n | solution.py:118
  36.2 1.0 %copy.43 = bf16[512,512]{0,1:T(8,128)(2,1)} copy(bf16[512,512]{1,0:T(8,128)(2,1)S(1)} %get-tuple-element.5) | data formatting | bytes 1048576 | tf_op jit(solution)/shard_map/slice | solution.py:80
  37.2 1.3 %copy.42 = bf16[512,512]{0,1:T(8,128)(2,1)S(1)} copy(bf16[512,512]{1,0:T(8,128)(2,1)} %get-tuple-element.4) | data formatting | bytes 1048576 | tf_op jit(solution)/shard_map/slice | solution.py:78
  38.5 1.4 %multiply_reduce_fusion = (f32[16,256]{1,0:T(8,128)S(1)}, f32[16,256,512]{2,1,0:T(8,128)S(1)}) fusion(bf16[256,16,32]{0,2,1:T(8,128)(2,1)S(1)} %bitcast.50, bf16[512,16,32]{0,2,1:T(8,128)(2,1)S(1)} %bitcast.47), kind=kOutput, calls=%fused_computation.5 | convolution fusion | flops 138407936 | bytes 9191424 | tf_op jit(solution)/shard_map/nhd,whd->hnw/dot_general | solution.py:82
  39.9 2.0 %fusion.2 = f32[16,256]{1,0:T(8,128)S(1)} fusion(f32[16,256,512]{2,1,0:T(8,128)S(1)} %get-tuple-element.13, f32[16,256]{1,0:T(8,128)S(1)} %get-tuple-element.12), kind=kLoop, calls=%fused_computation.6 | loop fusion | flops 6287360 | bytes 8421376 | tf_op jit(solution)/shard_map/reduce_sum | solution.py:83
  41.9 2.6 %fusion.30 = bf16[16,256,32]{1,2,0:T(8,128)(2,1)S(1)} fusion(bf16[512,16,32]{0,2,1:T(8,128)(2,1)S(1)} %bitcast.53, f32[16,256,512]{2,1,0:T(8,128)S(1)} %get-tuple-element.13, f32[16,256]{1,0:T(8,128)S(1)} %fusion.2, f32[16,256]{1,0:T(8,128)S(1)} %get-tuple-element.12), kind=kOutput, calls=%fused_computation.47 | convolution fusion | flops 140640256 | bytes 9207808 | tf_op jit(solution)/shard_map/hnw,whd->hnd/dot_general | solution.py:84
  44.9 2.4 %collective-permute-start.4 = (bf16[256,512]{1,0:T(8,128)(2,1)S(1)}, bf16[256,512]{1,0:T(8,128)(2,1)S(1)}, u32[]{:S(2)}, u32[]{:S(2)}) collective-permute-start(bf16[256,512]{1,0:T(8,128)(2,1)S(1)} %fusion.29), channel_id=1, source_target_pairs={{1,0},{2,1},{3,2},{4,3},{5,4},{6,5},{7,6},{8,7},{9,8},{10,9},{11,1... | collective-permute-start | bytes 786440 | tf_op jit(solution)/shard_map/ppermute | solution.py:20
  47.3 4.1 %collective-permute-start.3 = (bf16[256,512]{1,0:T(8,128)(2,1)S(1)}, bf16[256,512]{1,0:T(8,128)(2,1)S(1)}, u32[]{:S(2)}, u32[]{:S(2)}) collective-permute-start(bf16[256,512]{1,0:T(8,128)(2,1)S(1)} %fusion.29), channel_id=1, source_target_pairs={{0,1},{1,2},{2,3},{3,4},{4,5},{5,6},{6,7},{7,8},{8,9},{9,10},{10,1... | collective-permute-start | bytes 786440 | tf_op jit(solution)/shard_map/ppermute | solution.py:19
  53.3 3.2 %collective-permute-done.3 = bf16[256,512]{1,0:T(8,128)(2,1)S(1)} collective-permute-done((bf16[256,512]{1,0:T(8,128)(2,1)S(1)}, bf16[256,512]{1,0:T(8,128)(2,1)S(1)}, u32[]{:S(2)}, u32[]{:S(2)}) %collective-permute-start.3) | collective-permute-done | bytes 262176 | tf_op jit(solution)/shard_map/ppermute | solution.py:19
  57.1 2.3 %convolution_convert_fusion.1 = bf16[768,1024]{1,0:T(8,128)(2,1)S(1)} fusion(bf16[512,1536]{1,0:T(8,128)(2,1)} %param.20, f32[768]{0:T(1024)S(1)} %add_rsqrt_fusion, f32[768]{0:T(1024)S(1)} %broadcast_multiply_fusion, bf16[256,512]{1,0:T(8,128)(2,1)S(1)} %collective-permute-done.4, bf16[256,512]{1,0:T(8,128)(2,1)S(1)} %fusion.29, ...), kind=kOutput, calls=%fused_computation.35 | convolution fusion | flops 809631744 | bytes 3414016 | tf_op jit(solution)/shard_map/dot_general | solution.py:37
  59.3 1.0 %fusion.90 = (bf16[768,512]{1,0:T(8,128)(2,1)S(1)}, bf16[768,512]{1,0:T(8,128)(2,1)}) fusion(bf16[768,1024]{1,0:T(8,128)(2,1)S(1)} %convolution_convert_fusion.1), kind=kLoop, calls=%fused_computation.128 | loop fusion | bytes 3145728 | tf_op jit(solution)/shard_map/slice | solution.py:51
  60.4 2.3 %copy.45 = bf16[768,512]{0,1:T(8,128)(2,1)} copy(bf16[768,512]{1,0:T(8,128)(2,1)} %get-tuple-element.3) | data formatting | bytes 1572864 | tf_op jit(solution)/shard_map/slice | solution.py:53
  62.7 1.2 %copy.44 = bf16[768,512]{0,1:T(8,128)(2,1)} copy(bf16[768,512]{1,0:T(8,128)(2,1)S(1)} %get-tuple-element.2) | data formatting | bytes 1572864 | tf_op jit(solution)/shard_map/slice | solution.py:51
  63.8 2.5 %fusion.4 = (f32[16,128]{1,0:T(8,128)S(1)}, f32[16,128,768]{2,1,0:T(8,128)S(1)}) fusion(pred[128,768]{1,0:T(8,128)(4,1)} %broadcast_compare_fusion.1, bf16[128,16,32]{0,2,1:T(8,128)(2,1)} %bitcast.52, bf16[768,16,32]{0,2,1:T(8,128)(2,1)} %bitcast.46), kind=kOutput, calls=%fused_computation.12 | convolution fusion | flops 105379840 | bytes 7315456 | tf_op jit(solution)/shard_map/nhd,chd->hnc/dot_general | solution.py:55
  66.4 1.9 %fusion.7 = f32[16,128]{1,0:T(8,128)S(1)} fusion(f32[16,128,768]{2,1,0:T(8,128)S(1)} %get-tuple-element.15, f32[16,128]{1,0:T(8,128)S(1)} %get-tuple-element.14, f32[128,768]{1,0:T(8,128)S(1)} %convert_reduce_fusion.2, pred[128,768]{1,0:T(8,128)(4,1)S(1)} %copy-done.6), kind=kLoop, calls=%fused_computation.15 | loop fusion | flops 7862272 | bytes 6799360 | tf_op jit(solution)/shard_map/reduce_sum | solution.py:61
  68.3 2.1 %fusion.38 = bf16[128,16,32]{0,2,1:T(8,128)(2,1)S(1)} fusion(bf16[768,16,32]{0,2,1:T(8,128)(2,1)S(1)} %bitcast.51, f32[16,128,768]{2,1,0:T(8,128)S(1)} %get-tuple-element.15, f32[16,128]{1,0:T(8,128)S(1)} %get-tuple-element.14, f32[128,768]{1,0:T(8,128)S(1)} %convert_reduce_fusion.2, pred[128,768]{1,0:T(8,128)(4,1)S(1)} %copy-done.6, f32[128,16]{0,1:T(8,128)S(1)} %bitcast.59), kind=kOutput, calls=%fused_computation.58 | convolution fusion | flops 107085824 | bytes 7716864 | tf_op jit(solution)/shard_map/hnc,chd->hnd/dot_general | solution.py:62
  71.0 3.2 %fusion.36 = bf16[128,512]{1,0:T(8,128)(2,1)} fusion(f32[128,512]{1,0:T(8,128)S(1)} %get-tuple-element.17, bf16[2048,512]{1,0:T(8,128)(2,1)S(1)} %copy-done, bf16[512,2048]{1,0:T(8,128)(2,1)} %param.22, f32[128]{0:T(128)S(1)} %add_rsqrt_fusion.3, f32[128]{0:T(128)S(1)} %broadcast_multiply_fusion.3), kind=kOutput, calls=%fused_computation.55 | convolution fusion | flops 539557888 | bytes 4588544 | tf_op jit(solution)/shard_map/dot_general | solution.py:37
  (69 shorter events, 10.0 us)
Async XLA Ops:
  0.6 70.4 %copy-start = (bf16[2048,512]{1,0:T(8,128)(2,1)S(1)}, bf16[2048,512]{1,0:T(8,128)(2,1)}, u32[]{:S(2)}) copy-start(bf16[2048,512]{1,0:T(8,128)(2,1)} %param.23) | copy-start | bytes 6291460
  4.6 14.1 %collective-permute-start.1 = (bf16[128,1024]{1,0:T(8,128)(2,1)S(1)}, bf16[128,1024]{1,0:T(8,128)(2,1)S(1)}, u32[]{:S(2)}, u32[]{:S(2)}) collective-permute-start(bf16[128,1024]{1,0:T(8,128)(2,1)S(1)} %convolution_convert_fusion.2), channel_id=1, source_target_pairs={{1,0},{2,1},{3,2},{4,3},{5,4},{6,5},{7,6},{8,7},{9,8},{10,9},{11,1... | collective-permute-start | bytes 786440 | tf_op jit(solution)/shard_map/ppermute | solution.py:20
  6.5 12.1 %collective-permute-start = (bf16[128,1024]{1,0:T(8,128)(2,1)S(1)}, bf16[128,1024]{1,0:T(8,128)(2,1)}, u32[]{:S(2)}, u32[]{:S(2)}) collective-permute-start(bf16[128,1024]{1,0:T(8,128)(2,1)S(1)} %convolution_convert_fusion.2), channel_id=1, source_target_pairs={{0,1},{1,2},{2,3},{3,4},{4,5},{5,6},{6,7},{7,8},{8,9},{9,10},{10,1... | collective-permute-start | bytes 786440 | tf_op jit(solution)/shard_map/ppermute | solution.py:19
  20.8 2.3 %copy-start.7 = (pred[256,384]{1,0:T(8,128)(4,1)S(1)}, pred[256,384]{1,0:T(8,128)(4,1)}, u32[]{:S(2)}) copy-start(pred[256,384]{1,0:T(8,128)(4,1)} %broadcast_compare_fusion) | copy-start | bytes 294916
  20.9 4.4 %copy-start.13 = (bf16[384,512]{0,1:T(8,128)(2,1)S(1)}, bf16[384,512]{0,1:T(8,128)(2,1)}, u32[]{:S(2)}) copy-start(bf16[384,512]{0,1:T(8,128)(2,1)} %copy.40) | copy-start | bytes 1179652
  25.3 2.1 %copy-start.2 = (bf16[256,512]{1,0:T(8,128)(2,1)S(1)}, bf16[256,512]{1,0:T(8,128)(2,1)}, u32[]{:S(2)}) copy-start(bf16[256,512]{1,0:T(8,128)(2,1)} %param.13) | copy-start | bytes 786436
  25.3 2.1 %copy-start.12 = (bf16[512,512]{1,0:T(8,128)(2,1)S(1)}, bf16[512,512]{1,0:T(8,128)(2,1)}, u32[]{:S(2)}) copy-start(bf16[512,512]{1,0:T(8,128)(2,1)} %param.17) | copy-start | bytes 1572868
  25.3 2.7 %copy-start.3 = (bf16[512,1536]{1,0:T(8,128)(2,1)S(1)}, bf16[512,1536]{1,0:T(8,128)(2,1)}, u32[]{:S(2)}) copy-start(bf16[512,1536]{1,0:T(8,128)(2,1)} %param.18) | copy-start | bytes 4718596
  25.3 4.2 %copy-start.15 = (s32[128,3]{0,1:T(4,128)S(1)}, s32[128,3]{0,1:T(4,128)}, u32[]{:S(2)}) copy-start(s32[128,3]{0,1:T(4,128)} %param.15) | copy-start | bytes 4612
  25.3 4.2 %copy-start.4 = (bf16[128,512]{1,0:T(8,128)(2,1)S(1)}, bf16[128,512]{1,0:T(8,128)(2,1)}, u32[]{:S(2)}) copy-start(bf16[128,512]{1,0:T(8,128)(2,1)} %param.12) | copy-start | bytes 393220
  29.5 3.8 %collective-permute-start.2 = (bf16[256,1024]{1,0:T(8,128)(2,1)}, bf16[256,1024]{1,0:T(8,128)(2,1)}, u32[]{:S(2)}, u32[]{:S(2)}) collective-permute-start(bf16[256,1024]{1,0:T(8,128)(2,1)} %slice.51), channel_id=1, source_target_pairs={{0,1},{1,0},{2,3},{3,2},{4,5},{5,4},{6,7},{7,6},{8,9},{9,8},{10,11... | collective-permute-start | bytes 1572872 | tf_op jit(solution)/shard_map/ppermute | solution.py:26
  39.9 2.0 %copy-start.10 = (bf16[512,512]{0,1:T(8,128)(2,1)S(1)}, bf16[512,512]{0,1:T(8,128)(2,1)}, u32[]{:S(2)}) copy-start(bf16[512,512]{0,1:T(8,128)(2,1)} %copy.43) | copy-start | bytes 1572868
  41.9 2.7 %copy-start.9 = (bf16[512,512]{1,0:T(8,128)(2,1)S(1)}, bf16[512,512]{1,0:T(8,128)(2,1)}, u32[]{:S(2)}) copy-start(bf16[512,512]{1,0:T(8,128)(2,1)} %param.19) | copy-start | bytes 1572868
  41.9 9.7 %copy-start.14 = (bf16[128,512]{1,0:T(8,128)(2,1)S(1)}, bf16[128,512]{1,0:T(8,128)(2,1)}, u32[]{:S(2)}) copy-start(bf16[128,512]{1,0:T(8,128)(2,1)} %convolution_convert_fusion.4) | copy-start | bytes 393220
  44.9 17.8 %copy-start.1 = (bf16[256,512]{1,0:T(8,128)(2,1)}, bf16[256,512]{1,0:T(8,128)(2,1)S(1)}, u32[]{:S(2)}) copy-start(bf16[256,512]{1,0:T(8,128)(2,1)S(1)} %fusion.29) | copy-start | bytes 786436
  44.9 8.4 %collective-permute-start.4 = (bf16[256,512]{1,0:T(8,128)(2,1)S(1)}, bf16[256,512]{1,0:T(8,128)(2,1)S(1)}, u32[]{:S(2)}, u32[]{:S(2)}) collective-permute-start(bf16[256,512]{1,0:T(8,128)(2,1)S(1)} %fusion.29), channel_id=1, source_target_pairs={{1,0},{2,1},{3,2},{4,3},{5,4},{6,5},{7,6},{8,7},{9,8},{10,9},{11,1... | collective-permute-start | bytes 786440 | tf_op jit(solution)/shard_map/ppermute | solution.py:20
  47.3 9.2 %collective-permute-start.3 = (bf16[256,512]{1,0:T(8,128)(2,1)S(1)}, bf16[256,512]{1,0:T(8,128)(2,1)S(1)}, u32[]{:S(2)}, u32[]{:S(2)}) collective-permute-start(bf16[256,512]{1,0:T(8,128)(2,1)S(1)} %fusion.29), channel_id=1, source_target_pairs={{0,1},{1,2},{2,3},{3,4},{4,5},{5,6},{6,7},{7,8},{8,9},{9,10},{10,1... | collective-permute-start | bytes 786440 | tf_op jit(solution)/shard_map/ppermute | solution.py:19
  62.7 3.7 %copy-start.6 = (pred[128,768]{1,0:T(8,128)(4,1)S(1)}, pred[128,768]{1,0:T(8,128)(4,1)}, u32[]{:S(2)}) copy-start(pred[128,768]{1,0:T(8,128)(4,1)} %broadcast_compare_fusion.1) | copy-start | bytes 294916
  63.8 4.5 %copy-start.8 = (bf16[768,512]{0,1:T(8,128)(2,1)S(1)}, bf16[768,512]{0,1:T(8,128)(2,1)}, u32[]{:S(2)}) copy-start(bf16[768,512]{0,1:T(8,128)(2,1)} %copy.45) | copy-start | bytes 2359300
  68.3 2.2 %copy-start.5 = (bf16[128,512]{1,0:T(8,128)(2,1)S(1)}, bf16[128,512]{1,0:T(8,128)(2,1)}, u32[]{:S(2)}) copy-start(bf16[128,512]{1,0:T(8,128)(2,1)} %param.12) | copy-start | bytes 393220
  68.3 2.1 %copy-start.11 = (bf16[512,512]{1,0:T(8,128)(2,1)S(1)}, bf16[512,512]{1,0:T(8,128)(2,1)}, u32[]{:S(2)}) copy-start(bf16[512,512]{1,0:T(8,128)(2,1)} %param.21) | copy-start | bytes 1572868
where the time goes:
time: 75 us; the launch traced here: 74.2 us
  matrix products  25.2 us (34%)
  other arithmetic  18.9 us (25%)
  starting transfers between devices  12.9 us (17%)
  local copies, waits for them, and re-layouts  12.6 us (17%)
  waiting for transfers between devices  3.44 us (5%)
  between operations  1.14 us (2%)
    dot_general x9, matrix products, product(): return jnp.dot(left, right, preferred_element_type=jnp.float32)  12.2 us
    ppermute x2, starting transfers between devices, padded(): before = lax.ppermute(last, axis, up)  8.55 us
    dot_general x2, matrix products, dense_partial(): jnp.einsum('nhd,chd->hnc', query_heads, key_heads, preferred_element_type...  4.83 us
    ppermute x2, starting transfers between devices, padded(): after = lax.ppermute(leading, axis, down)  4.34 us
    dot_general x2, matrix products, dense_partial(): jnp.einsum('hnc,chd->hnd', weights, value_heads, preferred_element_type=j...  4.16 us
    reduce_sum x2, other arithmetic, dense_partial(): totals = jnp.sum(weights, axis=-1)  3.98 us
    slice x2, local copies, waits for them, and re-layouts, dense_partial(): key_values[:, model_width:].astype(jnp.float32)  3.19 us
    ppermute x2, waiting for transfers between devices, padded(): before = lax.ppermute(last, axis, up)  3.16 us
  transfers between devices with their start and end apart: 5, of which 2 were waited for; matrix products, arithmetic and copies ran while one was open for 17% of the time, Pallas kernels for 0%

commit v1 on v0

v1 whole, which is shorter than its diff:
```python
import functools
import math

import jax
import jax.numpy as jnp
from jax import lax
from jax.experimental import pallas as pl
from jax.experimental.pallas import tpu as pltpu
from jax.sharding import PartitionSpec as P

HEADS = 16
EPSILON = 1e-05
LANES = 128
CHUNKS = 2
F32 = jnp.float32
BF16 = jnp.bfloat16
MESH = pl.DeviceIdType.MESH


def layer_norm(values):
    values = values.astype(F32)
    center = values - jnp.mean(values, axis=-1, keepdims=True)
    spread = jnp.mean(center * center, axis=-1, keepdims=True)
    return (center * lax.rsqrt(spread + EPSILON)).astype(BF16)


def product(left, right):
    return jnp.dot(left, right, preferred_element_type=F32)


def scores_of(left, right):
    return lax.dot_general(left, right, (((1,), (1,)), ((), ())), preferred_element_type=F32)


def head_masks(rows, head_size):
    lane = lax.broadcasted_iota(jnp.int32, (rows, LANES), 1)
    return [lane // head_size == h for h in range(LANES // head_size)]


def attend_group(queries, keys, values_ext, bias, masks):
    rows = queries.shape[0]
    stacked = jnp.concatenate([jnp.where(m, queries, jnp.zeros_like(queries)) for m in masks], axis=0)
    scores = scores_of(stacked, keys)
    if bias is not None:
        scores = (scores.reshape(len(masks), rows, -1) + bias[None]).reshape(scores.shape)
    maxima = jnp.max(scores, axis=-1, keepdims=True)
    weights = jnp.exp2(scores - maxima).astype(BF16)
    mixed = product(weights, values_ext)
    num = mixed[:rows, :LANES]
    den = mixed[:rows, LANES:]
    for h in range(1, len(masks)):
        part = mixed[h * rows : (h + 1) * rows]
        num = jnp.where(masks[h], part[:, :LANES], num)
        den = jnp.where(masks[h], part[:, LANES:], den)
    return num / den


def kernel(
    n,
    grid_hbm, hidden_hbm, enc_nbr_hbm, dec_nbr_hbm,
    enc_qkv_hbm, enc_out_hbm, proc_qkv_hbm, proc_out_hbm,
    dec_qkv_hbm, dec_out_hbm, mlp_in_hbm, mlp_out_hbm,
    grid_out_hbm, hidden_out_hbm,
    grid, hidden, enc_nbr, dec_nbr,
    enc_qkv, enc_out, proc_qkv, proc_out, dec_qkv, dec_out, mlp_in, mlp_out,
    grid_out, hidden_out,
    grid_l, grid_r, bias, enc_q, enc_k, enc_v,
    hidden_one, norm_one, norm_far, proc_q, proc_k, proc_v,
    norm_two, two_l, two_r, mix,
    load_sem, store_sem, send_sem, recv_sem,
):
    me = lax.axis_index("nodes")
    far = me + 1 - 2 * (me % 2)
    has_l = me > 0
    has_r = me < n - 1
    gb, width = grid.shape
    hb = hidden.shape[0]
    head_size = width // HEADS
    groups = width // LANES
    rows = hb // CHUNKS
    scale = math.log2(math.e) / math.sqrt(head_size)

    barrier = pltpu.get_barrier_semaphore()

    @pl.when(has_l)
    def _():
        pl.semaphore_signal(barrier, inc=1, device_id={"nodes": me - 1}, device_id_type=MESH)

    @pl.when(has_r)
    def _():
        pl.semaphore_signal(barrier, inc=1, device_id={"nodes": me + 1}, device_id_type=MESH)

    pairs = [
        (grid_hbm, grid), (hidden_hbm, hidden), (enc_nbr_hbm, enc_nbr), (enc_qkv_hbm, enc_qkv),
        (dec_nbr_hbm, dec_nbr), (enc_out_hbm, enc_out), (proc_qkv_hbm, proc_qkv), (proc_out_hbm, proc_out),
        (dec_qkv_hbm, dec_qkv), (dec_out_hbm, dec_out), (mlp_in_hbm, mlp_in), (mlp_out_hbm, mlp_out),
    ]
    loads = [pltpu.make_async_copy(s, d, load_sem.at[i]) for i, (s, d) in enumerate(pairs)]
    (ld_grid, ld_hidden, ld_enbr, ld_eqkv, ld_dnbr, ld_eout, ld_pqkv, ld_pout, ld_dqkv, ld_dout, ld_min, ld_mout) = loads
    for ld in (ld_grid, ld_hidden, ld_enbr, ld_eqkv):
        ld.start()

    def remote(src, dst, k, to):
        return pltpu.make_async_remote_copy(
            src_ref=src, dst_ref=dst, send_sem=send_sem.at[k], recv_sem=recv_sem.at[k],
            device_id={"nodes": to}, device_id_type=MESH,
        )

    grid_up = remote(grid_hbm, grid_l, 0, me + 1)
    grid_down = remote(grid_hbm, grid_r, 1, me - 1)

    pl.semaphore_wait(barrier, jnp.where(has_l, 1, 0) + jnp.where(has_r, 1, 0))

    @pl.when(has_r)
    def _():
        grid_up.start()

    @pl.when(has_l)
    def _():
        grid_down.start()

    @pl.when(jnp.logical_not(has_l))
    def _():
        grid_l[...] = jnp.zeros_like(grid_l)
        two_l[...] = jnp.zeros_like(two_l)

    @pl.when(jnp.logical_not(has_r))
    def _():
        grid_r[...] = jnp.zeros_like(grid_r)
        two_r[...] = jnp.zeros_like(two_r)

    for g in range(groups):
        enc_v[g, :, LANES:] = jnp.ones((3 * gb, LANES), BF16)
        proc_v[g, :, LANES:] = jnp.ones((2 * hb, LANES), BF16)

    ld_enbr.wait()
    base = (me - 1) * gb
    row = lax.broadcasted_iota(jnp.int32, (3 * gb, rows), 0) + base
    for c in range(CHUNKS):
        counts = jnp.zeros((3 * gb, rows), F32)
        for j in range(enc_nbr.shape[0]):
            counts = counts + jnp.where(enc_nbr[j : j + 1, c * rows : (c + 1) * rows] == row, 1.0, 0.0)
        logs = jnp.log(jnp.maximum(counts, 1.0)) * math.log2(math.e)
        bias[c * rows : (c + 1) * rows, :] = jnp.where(counts > 0.0, logs, -1e30).T

    ld_grid.wait()
    ld_hidden.wait()
    ld_eqkv.wait()
    for ld in (ld_eout, ld_pqkv, ld_pout, ld_dnbr, ld_dqkv, ld_dout):
        ld.start()

    def enc_pairs(block, source):
        normed = layer_norm(source[...])
        enc_k[block * gb : (block + 1) * gb, :] = product(normed, enc_qkv[:, width : 2 * width]).astype(BF16)
        values = product(normed, enc_qkv[:, 2 * width :]).astype(BF16)
        for g in range(groups):
            enc_v[g, block * gb : (block + 1) * gb, :LANES] = values[:, g * LANES : (g + 1) * LANES]
        return normed

    grid_normed = enc_pairs(1, grid)
    enc_q[...] = (product(layer_norm(hidden[...]), enc_qkv[:, :width]) * scale).astype(BF16)

    @pl.when(has_l)
    def _():
        grid_up.wait_recv()

    @pl.when(has_r)
    def _():
        grid_down.wait_recv()

    enc_pairs(0, grid_l)
    enc_pairs(2, grid_r)

    masks = head_masks(rows, head_size)
    ld_eout.wait()
    one_copies = []
    for c in range(CHUNKS):
        part = slice(c * rows, (c + 1) * rows)
        for g in range(groups):
            lanes = slice(g * LANES, (g + 1) * LANES)
            mix[:, lanes] = attend_group(
                enc_q[part, lanes], enc_k[:, lanes], enc_v[g], bias[part, :], masks
            ).astype(BF16)
        one = (hidden[part, :].astype(F32) + product(mix[...], enc_out[...])).astype(BF16)
        hidden_one[part, :] = one
        norm_one[part, :] = layer_norm(one)
        copy = remote(norm_one.at[pl.ds(c * rows, rows)], norm_far.at[pl.ds(c * rows, rows)], 2 + c, far)
        copy.start()
        one_copies.append(copy)

    ld_min.start()
    ld_mout.start()
    ld_pqkv.wait()

    def proc_pairs(block, source):
        normed = source[...]
        proc_k[block * hb : (block + 1) * hb, :] = product(normed, proc_qkv[:, width : 2 * width]).astype(BF16)
        values = product(normed, proc_qkv[:, 2 * width :]).astype(BF16)
        for g in range(groups):
            proc_v[g, block * hb : (block + 1) * hb, :LANES] = values[:, g * LANES : (g + 1) * LANES]

    proc_q[...] = (product(norm_one[...], proc_qkv[:, :width]) * scale).astype(BF16)
    proc_pairs(0, norm_one)
    for copy in one_copies:
        copy.wait_recv()
    proc_pairs(1, norm_far)
    ld_pout.wait()
    two_copies = []
    for c in range(CHUNKS):
        part = slice(c * rows, (c + 1) * rows)
        for g in range(groups):
            lanes = slice(g * LANES, (g + 1) * LANES)
            mix[:, lanes] = attend_group(
                proc_q[part, lanes], proc_k[:, lanes], proc_v[g], None, masks
            ).astype(BF16)
        two = (hidden_one[part, :].astype(F32) + product(mix[...], proc_out[...])).astype(BF16)
        hidden_out[part, :] = two
        norm_two[part, :] = layer_norm(two)
        view = pl.ds(c * rows, rows)
        up = remote(norm_two.at[view], two_l.at[view], 2 + CHUNKS + 2 * c, me + 1)
        down = remote(norm_two.at[view], two_r.at[view], 3 + CHUNKS + 2 * c, me - 1)

        @pl.when(has_r)
        def _():
            up.start()

        @pl.when(has_l)
        def _():
            down.start()

        two_copies.append((up, down))
    store_hidden = pltpu.make_async_copy(hidden_out, hidden_out_hbm, store_sem.at[0])
    store_hidden.start()

    ld_dnbr.wait()
    ld_dqkv.wait()
    dec_q = product(grid_normed, dec_qkv[:, :width]).astype(BF16).astype(F32)
    dec_lists = dec_nbr[...] - (me - 1) * hb
    slots = dec_lists.shape[0]
    row = lax.broadcasted_iota(jnp.int32, (hb, gb), 0)

    def gather(block, source):
        hot = jnp.concatenate(
            [jnp.where(dec_lists[j : j + 1, :] == row + block * hb, 1.0, 0.0) for j in range(slots)], axis=1
        ).astype(BF16)
        return lax.dot_general(hot, source[...], (((0,), (0,)), ((), ())), preferred_element_type=F32)

    gathered = gather(1, norm_two)
    for up, down in two_copies:

        @pl.when(has_l)
        def _():
            up.wait_recv()

        @pl.when(has_r)
        def _():
            down.wait_recv()

    gathered = (gathered + gather(0, two_l) + gather(2, two_r)).astype(BF16)
    dec_k = product(gathered, dec_qkv[:, width : 2 * width]).astype(BF16).astype(F32)
    dec_v = product(gathered, dec_qkv[:, 2 * width :]).astype(BF16).astype(F32)
    wide = 2 * LANES
    same = (
        lax.broadcasted_iota(jnp.int32, (wide, wide), 0) // head_size
        == lax.broadcasted_iota(jnp.int32, (wide, wide), 1) // head_size
    )
    same = jnp.where(same, 1.0, 0.0).astype(BF16)
    terms = jnp.concatenate([dec_q] * slots, axis=0) * dec_k
    high = terms.astype(BF16)
    low = (terms - high.astype(F32)).astype(BF16)
    sums = [
        product(high[:, i : i + wide], same) + product(low[:, i : i + wide], same) for i in range(0, width, wide)
    ]
    scores = jnp.concatenate(sums, axis=1) * scale
    tops = scores[:gb]
    for j in range(1, slots):
        tops = jnp.maximum(tops, scores[j * gb : (j + 1) * gb])
    total = jnp.zeros((gb, width), F32)
    mixed = jnp.zeros((gb, width), F32)
    for j in range(slots):
        weight = jnp.exp2(scores[j * gb : (j + 1) * gb] - tops)
        total = total + weight
        mixed = mixed + weight * dec_v[j * gb : (j + 1) * gb]
    dec_mix = (mixed / total).astype(BF16)
    ld_dout.wait()
    grid_one = (grid[...].astype(F32) + product(dec_mix, dec_out[...])).astype(BF16)
    normed = layer_norm(grid_one)
    ld_min.wait()
    units = jax.nn.gelu(product(normed, mlp_in[...])).astype(BF16)
    ld_mout.wait()
    grid_out[...] = (grid_one.astype(F32) + product(units, mlp_out[...])).astype(BF16)
    store_grid = pltpu.make_async_copy(grid_out, grid_out_hbm, store_sem.at[1])
    store_grid.start()

    for copy in one_copies:
        copy.wait_send()

    @pl.when(has_r)
    def _():
        grid_up.wait_send()
        for up, _ in two_copies:
            up.wait_send()

    @pl.when(has_l)
    def _():
        grid_down.wait_send()
        for _, down in two_copies:
            down.wait_send()

    store_hidden.wait()
    store_grid.wait()


def local(*args):
    args = args[:2] + (args[2].T, args[3].T) + args[4:]
    grid, hidden = args[:2]
    gb, width = grid.shape
    hb = hidden.shape[0]
    groups = width // LANES
    n = lax.axis_size("nodes")
    vmem = [pltpu.VMEM(a.shape, a.dtype) for a in args]
    scratch = vmem + [
        pltpu.VMEM(grid.shape, BF16),
        pltpu.VMEM(hidden.shape, BF16),
        pltpu.VMEM(grid.shape, BF16),
        pltpu.VMEM(grid.shape, BF16),
        pltpu.VMEM((hb, 3 * gb), F32),
        pltpu.VMEM(hidden.shape, BF16),
        pltpu.VMEM((3 * gb, width), BF16),
        pltpu.VMEM((groups, 3 * gb, 2 * LANES), BF16),
        pltpu.VMEM(hidden.shape, BF16),
        pltpu.VMEM(hidden.shape, BF16),
        pltpu.VMEM(hidden.shape, BF16),
        pltpu.VMEM(hidden.shape, BF16),
        pltpu.VMEM((2 * hb, width), BF16),
        pltpu.VMEM((groups, 2 * hb, 2 * LANES), BF16),
        pltpu.VMEM(hidden.shape, BF16),
        pltpu.VMEM(hidden.shape, BF16),
        pltpu.VMEM(hidden.shape, BF16),
        pltpu.VMEM((hb // CHUNKS, width), BF16),
        pltpu.SemaphoreType.DMA((len(args),)),
        pltpu.SemaphoreType.DMA((2,)),
        pltpu.SemaphoreType.DMA((2 + 3 * CHUNKS,)),
        pltpu.SemaphoreType.DMA((2 + 3 * CHUNKS,)),
    ]
    return pl.pallas_call(
        functools.partial(kernel, n),
        out_shape=(jax.ShapeDtypeStruct(grid.shape, BF16), jax.ShapeDtypeStruct(hidden.shape, BF16)),
        in_specs=[pl.BlockSpec(memory_space=pl.ANY)] * len(args),
        out_specs=(pl.BlockSpec(memory_space=pl.ANY), pl.BlockSpec(memory_space=pl.ANY)),
        scratch_shapes=scratch,
        compiler_params=pltpu.CompilerParams(collective_id=0, has_side_effects=True, vmem_limit_bytes=60 * 2**20),
        name="layer",
    )(*args)


def solution(mesh):
    spread = P(("groups", "nodes"), None)
    return jax.shard_map(
        local,
        mesh=mesh,
        in_specs=(spread, spread, P("nodes", None), P("nodes", None)) + (P(),) * 8,
        out_specs=(spread, spread),
        check_vma=False,
    )
```

time: 75 us -> 30 us (0.40)
  the two profiles are of different devices: /device:TPU:1 before, /device:TPU:17 now
where the time goes in v1:
time: 30 us; the launch traced here: 29.8 us
  Pallas kernels  25.9 us (86%)
  local copies, waits for them, and re-layouts  3.24 us (11%)
  between operations  0.64 us (2%)
    pallas_call x1, Pallas kernels, local(): pl.pallas_call(functools.partial(kernel, n), out_shape=(jax.ShapeDtypeStr...  25.9 us
    unnamed x2, local copies, waits for them, and re-layouts  3.24 us

profile of v1, /device:TPU:17, one launch (start us, length us, event | category | flops | bytes accessed | tf_op | source)
XLA Modules:
  0.0 29.8 jit_solution(10881436665000118180)
XLA Ops:
  0.6 25.9 %layer.1 = (bf16[128,512]{1,0:T(8,128)(2,1)}, bf16[256,512]{1,0:T(8,128)(2,1)}) custom-call(bf16[128,512]{1,0:T(8,128)(2,1)} %grid_hbm.1, bf16[256,512]{1,0:T(8,128)(2,1)} %hidden_hbm.1, s32[32,256]{1,0:T(8,128)} %bitcast.2, s32[3,128]{1,0:T(4,128)} %bitcast.3, bf16[512,1536]{1,0:T(8,128)(2,1)} %enc_qkv_hbm.1, bf16[512,512]{1,0:T(8,128)(2,1)} %enc_out_hbm.1, ...), custom_call_target="tpu_custom_call" | custom-call | tf_op jit(solution)/shard_map/layer/pallas_call | solution.py:346
  26.6 1.6 %copy.16 = bf16[128,512]{1,0:T(8,128)(2,1)} copy(bf16[128,512]{1,0:T(8,128)(2,1)} %get-tuple-element.4) | data formatting | bytes 262144
  28.2 1.7 %copy.17 = bf16[256,512]{1,0:T(8,128)(2,1)} copy(bf16[256,512]{1,0:T(8,128)(2,1)} %get-tuple-element.5) | data formatting | bytes 524288

commit v2 on v1

--- a/solution.py
+++ b/solution.py
@@ -37,22 +37,33 @@
     return [lane // head_size == h for h in range(LANES // head_size)]
 
 
-def attend_group(queries, keys, values_ext, bias, masks):
-    rows = queries.shape[0]
-    stacked = jnp.concatenate([jnp.where(m, queries, jnp.zeros_like(queries)) for m in masks], axis=0)
-    scores = scores_of(stacked, keys)
-    if bias is not None:
-        scores = (scores.reshape(len(masks), rows, -1) + bias[None]).reshape(scores.shape)
-    maxima = jnp.max(scores, axis=-1, keepdims=True)
-    weights = jnp.exp2(scores - maxima).astype(BF16)
-    mixed = product(weights, values_ext)
-    num = mixed[:rows, :LANES]
-    den = mixed[:rows, LANES:]
-    for h in range(1, len(masks)):
-        part = mixed[h * rows : (h + 1) * rows]
-        num = jnp.where(masks[h], part[:, :LANES], num)
-        den = jnp.where(masks[h], part[:, LANES:], den)
+def stacked_scores(queries, keys, masks):
+    return scores_of(jnp.concatenate([jnp.where(m, queries, jnp.zeros_like(queries)) for m in masks], axis=0), keys)
+
+
+def attend_rows(scores, values_ext, bias, masks):
+    rows = scores.shape[0] // len(masks)
+    num = den = None
+    for h, mask in enumerate(masks):
+        mine = scores[h * rows : (h + 1) * rows]
+        if bias is not None:
+            mine = mine + bias
+        weights = jnp.exp2(mine - jnp.max(mine, axis=-1, keepdims=True)).astype(BF16)
+        part = product(weights, values_ext)
+        num = part[:, :LANES] if h == 0 else jnp.where(mask, part[:, :LANES], num)
+        den = part[:, LANES:] if h == 0 else jnp.where(mask, part[:, LANES:], den)
     return num / den
+
+
+def attend_all(queries, keys, values_ext, bias, masks, mix):
+    groups = values_ext.shape[0]
+    lanes = [slice(g * LANES, (g + 1) * LANES) for g in range(groups)]
+    ahead = stacked_scores(queries[:, lanes[0]], keys[:, lanes[0]], masks)
+    for g in range(groups):
+        scores = ahead
+        if g + 1 < groups:
+            ahead = stacked_scores(queries[:, lanes[g + 1]], keys[:, lanes[g + 1]], masks)
+        mix[:, lanes[g]] = attend_rows(scores, values_ext[g], bias, masks).astype(BF16)
 
 
 def kernel(
@@ -60,14 +71,13 @@
     grid_hbm, hidden_hbm, enc_nbr_hbm, dec_nbr_hbm,
     enc_qkv_hbm, enc_out_hbm, proc_qkv_hbm, proc_out_hbm,
     dec_qkv_hbm, dec_out_hbm, mlp_in_hbm, mlp_out_hbm,
-    grid_out_hbm, hidden_out_hbm,
+    grid_out, hidden_out,
     grid, hidden, enc_nbr, dec_nbr,
     enc_qkv, enc_out, proc_qkv, proc_out, dec_qkv, dec_out, mlp_in, mlp_out,
-    grid_out, hidden_out,
     grid_l, grid_r, bias, enc_q, enc_k, enc_v,
     hidden_one, norm_one, norm_far, proc_q, proc_k, proc_v,
     norm_two, two_l, two_r, mix,
-    load_sem, store_sem, send_sem, recv_sem,
+    load_sem, send_sem, recv_sem,
 ):
     me = lax.axis_index("nodes")
     far = me + 1 - 2 * (me % 2)
@@ -135,13 +145,15 @@
 
     ld_enbr.wait()
     base = (me - 1) * gb
-    row = lax.broadcasted_iota(jnp.int32, (3 * gb, rows), 0) + base
+    row = lax.broadcasted_iota(jnp.int32, (gb, rows), 0) + base
     for c in range(CHUNKS):
-        counts = jnp.zeros((3 * gb, rows), F32)
-        for j in range(enc_nbr.shape[0]):
-            counts = counts + jnp.where(enc_nbr[j : j + 1, c * rows : (c + 1) * rows] == row, 1.0, 0.0)
-        logs = jnp.log(jnp.maximum(counts, 1.0)) * math.log2(math.e)
-        bias[c * rows : (c + 1) * rows, :] = jnp.where(counts > 0.0, logs, -1e30).T
+        for block in range(3):
+            counts = jnp.zeros((gb, rows), F32)
+            for j in range(enc_nbr.shape[0]):
+                mine = enc_nbr[j : j + 1, c * rows : (c + 1) * rows] - block * gb
+                counts = counts + jnp.where(mine == row, 1.0, 0.0)
+            logs = jnp.log(jnp.maximum(counts, 1.0)) * math.log2(math.e)
+            bias[c * rows : (c + 1) * rows, block * gb : (block + 1) * gb] = jnp.where(counts > 0.0, logs, -1e30).T
 
     ld_grid.wait()
     ld_hidden.wait()
@@ -176,11 +188,7 @@
     one_copies = []
     for c in range(CHUNKS):
         part = slice(c * rows, (c + 1) * rows)
-        for g in range(groups):
-            lanes = slice(g * LANES, (g + 1) * LANES)
-            mix[:, lanes] = attend_group(
-                enc_q[part, lanes], enc_k[:, lanes], enc_v[g], bias[part, :], masks
-            ).astype(BF16)
+        attend_all(enc_q.at[part], enc_k, enc_v, bias[part, :], masks, mix)
         one = (hidden[part, :].astype(F32) + product(mix[...], enc_out[...])).astype(BF16)
         hidden_one[part, :] = one
         norm_one[part, :] = layer_norm(one)
@@ -192,27 +200,23 @@
     ld_mout.start()
     ld_pqkv.wait()
 
-    def proc_pairs(block, source):
-        normed = source[...]
-        proc_k[block * hb : (block + 1) * hb, :] = product(normed, proc_qkv[:, width : 2 * width]).astype(BF16)
+    def proc_pairs(first, normed):
+        place = slice(first, first + normed.shape[0])
+        proc_k[place, :] = product(normed, proc_qkv[:, width : 2 * width]).astype(BF16)
         values = product(normed, proc_qkv[:, 2 * width :]).astype(BF16)
         for g in range(groups):
-            proc_v[g, block * hb : (block + 1) * hb, :LANES] = values[:, g * LANES : (g + 1) * LANES]
+            proc_v[g, place, :LANES] = values[:, g * LANES : (g + 1) * LANES]
 
     proc_q[...] = (product(norm_one[...], proc_qkv[:, :width]) * scale).astype(BF16)
-    proc_pairs(0, norm_one)
-    for copy in one_copies:
+    proc_pairs(0, norm_one[...])
+    for c, copy in enumerate(one_copies):
         copy.wait_recv()
-    proc_pairs(1, norm_far)
+        proc_pairs(hb + c * rows, norm_far[c * rows : (c + 1) * rows, :])
     ld_pout.wait()
     two_copies = []
     for c in range(CHUNKS):
         part = slice(c * rows, (c + 1) * rows)
-        for g in range(groups):
-            lanes = slice(g * LANES, (g + 1) * LANES)
-            mix[:, lanes] = attend_group(
-                proc_q[part, lanes], proc_k[:, lanes], proc_v[g], None, masks
-            ).astype(BF16)
+        attend_all(proc_q.at[part], proc_k, proc_v, None, masks, mix)
         two = (hidden_one[part, :].astype(F32) + product(mix[...], proc_out[...])).astype(BF16)
         hidden_out[part, :] = two
         norm_two[part, :] = layer_norm(two)
@@ -229,8 +233,6 @@
             down.start()
 
         two_copies.append((up, down))
-    store_hidden = pltpu.make_async_copy(hidden_out, hidden_out_hbm, store_sem.at[0])
-    store_hidden.start()
 
     ld_dnbr.wait()
     ld_dqkv.wait()
@@ -286,11 +288,15 @@
     grid_one = (grid[...].astype(F32) + product(dec_mix, dec_out[...])).astype(BF16)
     normed = layer_norm(grid_one)
     ld_min.wait()
-    units = jax.nn.gelu(product(normed, mlp_in[...])).astype(BF16)
     ld_mout.wait()
-    grid_out[...] = (grid_one.astype(F32) + product(units, mlp_out[...])).astype(BF16)
-    store_grid = pltpu.make_async_copy(grid_out, grid_out_hbm, store_sem.at[1])
-    store_grid.start()
+    ahead = product(normed, mlp_in[:, :width])
+    total = grid_one.astype(F32)
+    for i in range(0, mlp_in.shape[1], width):
+        now = ahead
+        if i + width < mlp_in.shape[1]:
+            ahead = product(normed, mlp_in[:, i + width : i + 2 * width])
+        total = total + product(jax.nn.gelu(now).astype(BF16), mlp_out[i : i + width, :])
+    grid_out[...] = total.astype(BF16)
 
     for copy in one_copies:
         copy.wait_send()
@@ -306,9 +312,6 @@
         grid_down.wait_send()
         for _, down in two_copies:
             down.wait_send()
-
-    store_hidden.wait()
-    store_grid.wait()
 
 
 def local(*args):
@@ -321,8 +324,6 @@
     vmem = [pltpu.VMEM(a.shape, a.dtype) for a in args]
     scratch = vmem + [
         pltpu.VMEM(grid.shape, BF16),
-        pltpu.VMEM(hidden.shape, BF16),
-        pltpu.VMEM(grid.shape, BF16),
         pltpu.VMEM(grid.shape, BF16),
         pltpu.VMEM((hb, 3 * gb), F32),
         pltpu.VMEM(hidden.shape, BF16),
@@ -339,19 +340,37 @@
         pltpu.VMEM(hidden.shape, BF16),
         pltpu.VMEM((hb // CHUNKS, width), BF16),
         pltpu.SemaphoreType.DMA((len(args),)),
-        pltpu.SemaphoreType.DMA((2,)),
         pltpu.SemaphoreType.DMA((2 + 3 * CHUNKS,)),
         pltpu.SemaphoreType.DMA((2 + 3 * CHUNKS,)),
     ]
-    return pl.pallas_call(
+    args = [pltpu.with_memory_space_constraint(a, pltpu.HBM) for a in args]
+    mid = pl.pallas_call(
         functools.partial(kernel, n),
         out_shape=(jax.ShapeDtypeStruct(grid.shape, BF16), jax.ShapeDtypeStruct(hidden.shape, BF16)),
         in_specs=[pl.BlockSpec(memory_space=pl.ANY)] * len(args),
-        out_specs=(pl.BlockSpec(memory_space=pl.ANY), pl.BlockSpec(memory_space=pl.ANY)),
+        out_specs=(pl.BlockSpec(memory_space=pltpu.VMEM), pl.BlockSpec(memory_space=pltpu.VMEM)),
         scratch_shapes=scratch,
-        compiler_params=pltpu.CompilerParams(collective_id=0, has_side_effects=True, vmem_limit_bytes=60 * 2**20),
+        compiler_params=pltpu.CompilerParams(collective_id=0, has_side_effects=True, vmem_limit_bytes=40 * 2**20),
         name="layer",
     )(*args)
+    return pl.pallas_call(
+        finish,
+        out_shape=(jax.ShapeDtypeStruct(grid.shape, BF16), jax.ShapeDtypeStruct(hidden.shape, BF16)),
+        in_specs=[pl.BlockSpec(memory_space=pl.ANY)] * 2,
+        out_specs=(pl.BlockSpec(memory_space=pl.ANY), pl.BlockSpec(memory_space=pl.ANY)),
+        scratch_shapes=[pltpu.SemaphoreType.DMA((2,))],
+        compiler_params=pltpu.CompilerParams(vmem_limit_bytes=2**20),
+        name="finish",
+    )(*mid)
+
+
+def finish(grid_mid, hidden_mid, grid_out, hidden_out, sem):
+    one = pltpu.make_async_copy(grid_mid, grid_out, sem.at[0])
+    two = pltpu.make_async_copy(hidden_mid, hidden_out, sem.at[1])
+    one.start()
+    two.start()
+    one.wait()
+    two.wait()
 
 
 def solution(mesh):

time: 30 us -> 25.5 us (0.85)
  local copies, waits for them, and re-layouts: 3.24 us -> 0 us
  Pallas kernels: 25.9 us -> 24.7 us
    unnamed x2 -> x0, local copies, waits for them, and re-layouts: 3.24 us -> none
    pallas_call x1, Pallas kernels: 25.9 us -> 24 us  [local(): pl.pallas_call(functools.partial(kernel, n), out_shape=(jax.ShapeDtypeStr...]
    pallas_call x0 -> x1, Pallas kernels: none -> 0.77 us  [local(): pl.pallas_call(finish, out_shape=(jax.ShapeDtypeStruct(grid.shape, BF16),...]
where the time goes in v2:
time: 25.5 us; the launch traced here: 25.4 us
  Pallas kernels  24.7 us (97%)
  between operations  0.64 us (3%)
    pallas_call x1, Pallas kernels, local(): pl.pallas_call(functools.partial(kernel, n), out_shape=(jax.ShapeDtypeStr...  24 us
    pallas_call x1, Pallas kernels, local(): pl.pallas_call(finish, out_shape=(jax.ShapeDtypeStruct(grid.shape, BF16),...  0.77 us

profile of v2, /device:TPU:17, one launch (start us, length us, event | category | flops | bytes accessed | tf_op | source)
XLA Modules:
  0.0 25.4 jit_solution(12138183607001617284)
XLA Ops:
  0.6 24.0 %layer.1 = (bf16[128,512]{1,0:T(8,128)(2,1)S(1)}, bf16[256,512]{1,0:T(8,128)(2,1)S(1)}) custom-call(bf16[128,512]{1,0:T(8,128)(2,1)} %grid_hbm.1, bf16[256,512]{1,0:T(8,128)(2,1)} %hidden_hbm.1, s32[32,256]{1,0:T(8,128)} %bitcast.2, s32[3,128]{1,0:T(4,128)} %bitcast.3, bf16[512,1536]{1,0:T(8,128)(2,1)} %enc_qkv_hbm.1, bf16[512,512]{1,0:T(8,128)(2,1)} %enc_out_hbm.1, ...), custom_call_target="tpu_custom_call" | custom-call | tf_op jit(solution)/shard_map/layer/pallas_call | solution.py:347
  24.6 0.8 %finish.1 = (bf16[128,512]{1,0:T(8,128)(2,1)}, bf16[256,512]{1,0:T(8,128)(2,1)}) custom-call(bf16[128,512]{1,0:T(8,128)(2,1)S(1)} %get-tuple-element.4.grid_mid, bf16[256,512]{1,0:T(8,128)(2,1)S(1)} %get-tuple-element.5.hidden_mid), custom_call_target="tpu_custom_call" | custom-call | tf_op jit(solution)/shard_map/finish/pallas_call | solution.py:356

commit v3 on v2

--- a/solution.py
+++ b/solution.py
@@ -241,14 +241,15 @@
     slots = dec_lists.shape[0]
     row = lax.broadcasted_iota(jnp.int32, (hb, gb), 0)
 
-    def gather(block, source):
-        hot = jnp.concatenate(
-            [jnp.where(dec_lists[j : j + 1, :] == row + block * hb, 1.0, 0.0) for j in range(slots)], axis=1
-        ).astype(BF16)
-        return lax.dot_general(hot, source[...], (((0,), (0,)), ((), ())), preferred_element_type=F32)
-
-    gathered = gather(1, norm_two)
-    for up, down in two_copies:
+    def hot(block):
+        per_slot = [
+            jnp.where(dec_lists[j : j + 1, :] == row + block * hb, 1.0, 0.0).T for j in range(slots)
+        ]
+        return jnp.concatenate(per_slot, axis=0).astype(BF16)
+
+    hot_l, hot_r = hot(0), hot(2)
+    gathered = product(hot(1), norm_two[...])
+    for c, (up, down) in enumerate(two_copies):
 
         @pl.when(has_l)
         def _():
@@ -258,7 +259,10 @@
         def _():
             down.wait_recv()
 
-    gathered = (gathered + gather(0, two_l) + gather(2, two_r)).astype(BF16)
+        part = slice(c * rows, (c + 1) * rows)
+        picks = jnp.concatenate([hot_l[:, part], hot_r[:, part]], axis=1)
+        gathered = gathered + product(picks, jnp.concatenate([two_l[part, :], two_r[part, :]], axis=0))
+    gathered = gathered.astype(BF16)
     dec_k = product(gathered, dec_qkv[:, width : 2 * width]).astype(BF16).astype(F32)
     dec_v = product(gathered, dec_qkv[:, 2 * width :]).astype(BF16).astype(F32)
     wide = 2 * LANES

time: 25.5 us -> 25.3 us (level)
  no operation moved by 1% of the time
where the time goes in v3:
time: 25.3 us; the launch traced here: 25.2 us
  Pallas kernels  24.5 us (97%)
  between operations  0.64 us (3%)
    pallas_call x1, Pallas kernels, local(): pl.pallas_call(functools.partial(kernel, n), out_shape=(jax.ShapeDtypeStr...  23.7 us
    pallas_call x1, Pallas kernels, local(): pl.pallas_call(finish, out_shape=(jax.ShapeDtypeStruct(grid.shape, BF16),...  0.77 us

profile of v3, /device:TPU:17, one launch (start us, length us, event | category | flops | bytes accessed | tf_op | source)
XLA Modules:
  0.0 25.2 jit_solution(3159282017431834576)
XLA Ops:
  0.6 23.7 %layer.1 = (bf16[128,512]{1,0:T(8,128)(2,1)S(1)}, bf16[256,512]{1,0:T(8,128)(2,1)S(1)}) custom-call(bf16[128,512]{1,0:T(8,128)(2,1)} %grid_hbm.1, bf16[256,512]{1,0:T(8,128)(2,1)} %hidden_hbm.1, s32[32,256]{1,0:T(8,128)} %bitcast.2, s32[3,128]{1,0:T(4,128)} %bitcast.3, bf16[512,1536]{1,0:T(8,128)(2,1)} %enc_qkv_hbm.1, bf16[512,512]{1,0:T(8,128)(2,1)} %enc_out_hbm.1, ...), custom_call_target="tpu_custom_call" | custom-call | tf_op jit(solution)/shard_map/layer/pallas_call | solution.py:351
  24.4 0.8 %finish.1 = (bf16[128,512]{1,0:T(8,128)(2,1)}, bf16[256,512]{1,0:T(8,128)(2,1)}) custom-call(bf16[128,512]{1,0:T(8,128)(2,1)S(1)} %get-tuple-element.4.grid_mid, bf16[256,512]{1,0:T(8,128)(2,1)S(1)} %get-tuple-element.5.hidden_mid), custom_call_target="tpu_custom_call" | custom-call | tf_op jit(solution)/shard_map/finish/pallas_call | solution.py:360
